TPU v7x, 128 devices: a whole 4x4x4 slice. The times are simulated.
128 devices in a mesh: req: 16 (over x, z), kv: 8 (over y, core).
Axes of the slice: x: 4, y: 4, z: 4, core: 2. Of those that a mesh axis runs over, the one named last changes fastest.
Arguments:
- residual_in: bfloat16 [512, 4096], P(None, 'req'), may hold values from -6 to 6
- attn_gain: float32 [4096], replicated, may hold values from 0.1 to 1.9
- query_weight: bfloat16 [4096, 4096], P(None, 'kv'), may hold values from -0.09375 to 0.09375
- key_matrix: bfloat16 [4096, 1024], P(None, 'kv'), may hold values from -0.09375 to 0.09375
- value_matrix: bfloat16 [4096, 1024], P(None, 'kv'), may hold values from -0.09375 to 0.09375
- key_cache: bfloat16 [512, 8, 640, 128], P('req', 'kv'), may hold values from -400 to 400
- cached_values: bfloat16 [512, 8, 640, 128], P('req', 'kv'), may hold values from -6 to 6
- cache_lengths: int32 [512], P('req'), may hold values from 1 to 640, as said below
- positions: int32 [512], P('req'), may hold values from 640 to 16383
- output_weight: bfloat16 [4096, 4096], P(None, 'req'), may hold values from -0.09375 to 0.09375
- mlp_gain: float32 [4096], P('req'), may hold values from 0.1 to 1.9
- gate_weight: bfloat16 [4096, 14336], P('req', 'kv'), may hold values from -0.09375 to 0.09375
- up_weight: bfloat16 [4096, 14336], P('req', 'kv'), may hold values from -0.09375 to 0.09375
- down_weight: bfloat16 [14336, 4096], P('kv', 'req'), may hold values from -0.046875 to 0.046875
Outputs:
- output: bfloat16 [512, 4096], P('kv', 'req')
Inputs may be any that keep to these rules, and one draw needn't show every extreme that they name: `cache_lengths`: each request's filled slots; some request has exactly 640 and some exactly 1.
All inputs are finite; a program needn't handle non-finite values.
Results may differ from a plain program's by a relative error of at most 0.025.
Values may be sent and summed in bfloat16 or wider, within the bound.
A program may use at most 128 MiB of HBM per device.

v0:
```python
import math
import jax
import jax.numpy as jnp
from jax import lax
from jax.sharding import PartitionSpec as P

MODEL_WIDTH = 4096
WINDOW = 512
SINKS = 4
EPS = 1e-05
THETA = 10000.0


def apply_rotary(vectors, places):
    half = vectors.shape[-1] // 2
    freqs = jnp.exp(
        jnp.arange(half, dtype=jnp.float32) * (-2.0 * math.log(THETA) / vectors.shape[-1])
    )
    angles = places.astype(jnp.float32)[:, None] * freqs[None, :]
    cosine = jnp.cos(angles)[:, None, :]
    sine = jnp.sin(angles)[:, None, :]
    first = vectors[..., :half]
    second = vectors[..., half:]
    return jnp.concatenate(
        [first * cosine - second * sine, second * cosine + first * sine], axis=-1
    )


def attend(query_rows, keys, values, new_key, new_value, allowed):
    factor = 1.0 / math.sqrt(query_rows.shape[-1])
    scores = (
        jnp.einsum("bgd,bjd->bgj", query_rows, keys, preferred_element_type=jnp.float32) * factor
    )
    scores = jnp.where(allowed[:, None, :], scores, -1e30)
    own = jnp.einsum("bgd,bd->bg", query_rows, new_key, preferred_element_type=jnp.float32) * factor
    peak = jnp.maximum(jnp.max(scores, axis=-1), own)
    expo = jnp.where(allowed[:, None, :], jnp.exp(scores - peak[..., None]), 0.0)
    own_expo = jnp.exp(own - peak)
    denom = jnp.sum(expo, axis=-1) + own_expo
    weights = (expo / denom[..., None]).astype(jnp.bfloat16)
    own_weight = (own_expo / denom).astype(jnp.bfloat16)
    mixed = jnp.einsum("bgj,bjd->bgd", weights, values, preferred_element_type=jnp.float32)
    mixed = (
        mixed
        + own_weight.astype(jnp.float32)[..., None] * new_value.astype(jnp.float32)[:, None, :]
    )
    return mixed.astype(jnp.bfloat16)


def shards(
    residual_in,
    attn_gain,
    query_weight,
    key_matrix,
    value_matrix,
    key_cache,
    cached_values,
    cache_lengths,
    positions,
    output_weight,
    mlp_gain,
    gate_weight,
    up_weight,
    down_weight,
):
    tokens = lax.all_to_all(residual_in, "req", split_axis=0, concat_axis=1, tiled=True)
    local_rows = tokens.shape[0]
    heads_here = key_cache.shape[1]
    head_size = key_cache.shape[3]
    query_group = query_weight.shape[1] // (heads_here * head_size)
    stream = tokens.astype(jnp.float32)
    normed_input = (
        stream
        / jnp.sqrt(jnp.sum(stream * stream, axis=-1, keepdims=True) / MODEL_WIDTH + EPS)
        * attn_gain
    ).astype(jnp.bfloat16)
    query_rows = jnp.dot(normed_input, query_weight, preferred_element_type=jnp.float32).reshape(
        local_rows, heads_here * query_group, head_size
    )
    query_rows = (
        apply_rotary(query_rows, positions)
        .astype(jnp.bfloat16)
        .reshape(local_rows, heads_here, query_group, head_size)
    )
    fresh_keys = jnp.dot(normed_input, key_matrix, preferred_element_type=jnp.float32).reshape(
        local_rows, heads_here, head_size
    )
    fresh_keys = apply_rotary(fresh_keys, positions).astype(jnp.bfloat16)
    fresh_values = (
        jnp.dot(normed_input, value_matrix, preferred_element_type=jnp.float32)
        .reshape(local_rows, heads_here, head_size)
        .astype(jnp.bfloat16)
    )
    slots = jnp.arange(key_cache.shape[2], dtype=jnp.int32)[None, :]
    limit = cache_lengths[:, None]
    allowed = (slots < limit) & ((slots < SINKS) | (slots > limit - WINDOW))
    results = [
        attend(
            query_rows[:, 0],
            key_cache[:, 0],
            cached_values[:, 0],
            fresh_keys[:, 0],
            fresh_values[:, 0],
            allowed,
        )
    ]
    attended_rows = jnp.stack(results, axis=1).reshape(
        local_rows, heads_here * query_group * head_size
    )
    features = attended_rows.shape[1]
    kv_place = lax.axis_index("kv")
    weight_rows = lax.dynamic_slice_in_dim(output_weight, kv_place * features, features, 0)
    partial_mix = jnp.dot(
        lax.all_gather(attended_rows, "req", axis=0, tiled=True),
        weight_rows,
        preferred_element_type=jnp.float32,
    )
    mixed = lax.psum(partial_mix.astype(jnp.bfloat16), "kv").astype(jnp.float32)
    middle = residual_in.astype(jnp.float32) + mixed
    scaled = (middle * mlp_gain).astype(jnp.bfloat16)
    squares = jnp.sum(middle * middle, axis=-1)
    gate_part = jnp.dot(scaled, gate_weight, preferred_element_type=jnp.float32)
    upper_part = jnp.dot(scaled, up_weight, preferred_element_type=jnp.float32)
    gate_total, upper_total, square_total = (
        lax.psum(gate_part.astype(jnp.bfloat16), "req").astype(jnp.float32),
        lax.psum(upper_part.astype(jnp.bfloat16), "req").astype(jnp.float32),
        lax.psum(squares.astype(jnp.bfloat16), "req").astype(jnp.float32),
    )
    inverse = (1.0 / jnp.sqrt(square_total / MODEL_WIDTH + EPS))[:, None]
    hidden = (jax.nn.silu(gate_total * inverse) * (upper_total * inverse)).astype(jnp.bfloat16)
    partial_out = jnp.dot(hidden, down_weight, preferred_element_type=jnp.float32)
    summed = lax.psum_scatter(
        partial_out.astype(jnp.bfloat16), "kv", scatter_dimension=0, tiled=True
    ).astype(jnp.float32)
    share = summed.shape[0]
    base_rows = lax.dynamic_slice_in_dim(middle, kv_place * share, share, 0)
    return (base_rows + summed).astype(jnp.bfloat16)


def solution(mesh):
    return jax.shard_map(
        shards,
        mesh=mesh,
        in_specs=(
            P(None, "req"),
            P(),
            P(None, "kv"),
            P(None, "kv"),
            P(None, "kv"),
            P("req", "kv", None, None),
            P("req", "kv", None, None),
            P("req"),
            P("req"),
            P(None, "req"),
            P("req"),
            P("req", "kv"),
            P("req", "kv"),
            P("kv", "req"),
        ),
        out_specs=P("kv", "req"),
        check_vma=False,
    )
```

profile of v0, /device:TPU:0, one launch (start us, length us, event | category | flops | bytes accessed | tf_op | source)
XLA Modules:
  0.0 266.5 jit_solution(15984500769440598371)
XLA Ops:
  6.5 0.0 copy-start
  6.5 8.1 %all-to-all-start = ((bf16[16,32,256]{2,1,0:T(8,128)(2,1)}), bf16[16,32,256]{2,1,0:T(8,128)(2,1)S(1)}, u32[]{:S(2)}, u32[]{:S(2)}) async-start(bf16[16,32,256]{2,1,0:T(8,128)(2,1)} %bitcast.48), calls=%async_computation | async-start | bytes 524288 | tf_op jit(solution)/shard_map/all_to_all | solution.py:66
  14.6 0.0 all-reduce.4.cloned.1.call-start
  14.7 0.7 broadcast_add_fusion
  15.4 0.7 fusion.29
  16.1 0.7 mul.176
  16.9 0.0 copy-start.10
  16.9 6.4 %copy.30 = bf16[512,4096]{1,0:T(8,128)(2,1)} copy(bf16[512,4096]{0,1:T(8,128)(2,1)} %bitcast.49) | data formatting | bytes 8388608 | tf_op jit(solution)/shard_map/dot_general | solution.py:77
  23.3 0.0 copy-done.10
  23.3 0.0 copy-start.7
  23.3 0.1 multiply_cosine_fusion.1
  23.5 0.0 all-to-all-done
  23.5 0.2 fusion.19
  23.7 0.1 fusion.22
  23.8 0.2 copy.24
  24.0 0.1 reshape.203
  24.1 0.0 copy-start.1
  24.2 0.0 copy-done.7
  24.2 0.0 copy-start.2
  24.2 1.7 convolution_bitcast_fusion
  25.9 0.1 fusion.45
  26.1 0.5 copy-done.1
  26.6 1.3 fusion.51
  27.9 0.0 copy-start.9
  28.0 0.1 subtract_convert_fusion
  28.1 0.1 pad_maximum_fusion
  28.1 0.1 maximum_bitcast_fusion
  28.2 0.1 fusion.31
  28.4 0.0 copy-done.2
  28.4 1.8 fusion.50
  30.2 0.3 fusion.24
  30.6 0.0 copy-done.9
  30.6 0.3 fusion.18
  30.9 0.0 copy-start.3
  30.9 0.0 copy-start.5
  30.9 0.0 copy-start.8
  30.9 3.6 %fusion.12 = bf16[32,4,128]{2,1,0:T(4,128)(2,1)S(1)} fusion(bf16[32,1,640,128]{3,2,1,0:T(8,128)(2,1)} %param.20, f32[32,4,640]{2,1,0:T(4,128)S(1)} %get-tuple-element.18, f32[32,4]{1,0:T(8,128)S(1)} %get-tuple-element.12, f32[32,4]{1,0:T(8,128)S(1)} %multiply_maximum_fusion, pred[32,640]{1,0:T(8,128)(4,1)S(1)} %fusion.29, f32[32,128]{1,0:T(8,128)S(1)} %fusion.18, ...), kind=kOutput, calls=%fused_computation.12 | convolution fusion | flops 21348352 | bytes 5641728 | tf_op jit(solution)/shard_map/bgj,bjd->bgd/dot_general | solution.py:42
  34.5 24.4 %all_gather.3 = bf16[512,512]{1,0:T(8,128)(2,1)S(1)} all-gather(bf16[32,512]{1,0:T(8,128)(2,1)S(1)} %bitcast.52), channel_id=1, replica_groups=mesh['req'=16,'kv'=8] {'req'}, dimensions={0}, use_global_device_ids=true | all-gather | bytes 557056 | tf_op jit(solution)/shard_map/all_gather | solution.py:114
  58.9 0.0 copy-done
  58.9 1.0 convolution_convert_fusion.2
  59.9 0.0 all-reduce.4.cloned.1.call-update
  60.0 0.0 all-reduce.6.cloned.1.call-start
  60.0 59.4 %all-reduce.4.cloned.1.call-done = bf16[512,256]{1,0:T(8,128)(2,1)} async-done(((bf16[512,256]{1,0:T(8,128)(2,1)}), bf16[512,256]{1,0:T(8,128)(2,1)}) %all-reduce.4.cloned.1.call-update) | async-done | bytes 262160 | tf_op jit(solution)/shard_map/psum | solution.py:118
  119.4 0.0 copy-done.3
  119.4 0.0 copy-done.5
  119.4 0.0 copy-done.8
  119.4 0.0 copy-start.6
  119.4 2.9 %convolution_convert_fusion = bf16[512,1792]{1,0:T(8,128)(2,1)} fusion(bf16[256,1792]{1,0:T(8,128)(2,1)S(1)} %copy-done.5, f32[256]{0:T(256)S(1)} %copy-done.8, bf16[512,256]{1,0:T(8,128)(2,1)} %all-reduce.4.cloned.1.call-done, bf16[512,256]{1,0:T(8,128)(2,1)S(1)} %copy-done.3), kind=kOutput, calls=%fused_computation.5 | convolution fusion | flops 471334912 | bytes 3277824 | tf_op jit(solution)/shard_map/dot_general | solution.py:123
  122.4 0.0 copy-done.6
  122.4 0.0 copy-start.4
  122.4 2.9 %convolution_convert_fusion.1 = bf16[512,1792]{1,0:T(8,128)(2,1)} fusion(bf16[256,1792]{1,0:T(8,128)(2,1)S(1)} %copy-done.6, f32[256]{0:T(256)S(1)} %copy-done.8, bf16[512,256]{1,0:T(8,128)(2,1)} %all-reduce.4.cloned.1.call-done, bf16[512,256]{1,0:T(8,128)(2,1)S(1)} %copy-done.3), kind=kOutput, calls=%fused_computation.6 | convolution fusion | flops 471334912 | bytes 3277824 | tf_op jit(solution)/shard_map/dot_general | solution.py:122
  125.3 0.0 all-reduce.6.cloned.1.call-update
  125.3 0.0 reduce-scatter.2.cloned.1.call-start
  125.4 0.0 copy-done.4
  125.4 0.2 convert_add_fusion
  125.5 41.1 %psum.30 = bf16[512]{0:T(512)(128)(2,1)S(1)} all-reduce(bf16[512]{0:T(512)(128)(2,1)S(1)} %get-tuple-element.8), channel_id=1, replica_groups=mesh['req'=16,'kv'=8] {'req'}, use_global_device_ids=true, to_apply=%region_6.7 | all-reduce | flops 512 | bytes 2048 | tf_op jit(solution)/shard_map/psum | solution.py:127
  166.7 57.5 %all-reduce.6.cloned.1.call-done = (bf16[512,1792]{1,0:T(8,128)(2,1)}, bf16[512,1792]{1,0:T(8,128)(2,1)}) async-done(((bf16[512,1792]{1,0:T(8,128)(2,1)}, bf16[512,1792]{1,0:T(8,128)(2,1)}), (bf16[512,1792]{1,0:T(8,128)(2,1)}, bf16[512,1792]{1,0:T(8,128)(2,1)})) %all-reduce.6.cloned.1.call-update) | async-done | bytes 3670032 | tf_op jit(solution)/shard_map/psum | solution.py:126
  224.2 4.4 %fusion.5 = bf16[512,256]{1,0:T(8,128)(2,1)} fusion(bf16[1792,256]{1,0:T(8,128)(2,1)} %param.27, bf16[512,1792]{1,0:T(8,128)(2,1)} %get-tuple-element.5, bf16[512,1792]{1,0:T(8,128)(2,1)} %get-tuple-element.6, f32[512]{0:T(512)S(1)} %add_rsqrt_fusion), kind=kOutput, calls=%fused_computation.9 | convolution fusion | flops 479068160 | bytes 4851712 | tf_op jit(solution)/shard_map/dot_general | solution.py:131
  228.6 0.0 reduce-scatter.2.cloned.1.call-update
  228.6 30.0 %reduce-scatter.2.cloned.1.call-done = bf16[64,256]{1,0:T(8,128)(2,1)} async-done(((bf16[512,256]{1,0:T(8,128)(2,1)}), bf16[64,256]{1,0:T(8,128)(2,1)}) %reduce-scatter.2.cloned.1.call-update) | async-done | bytes 32784 | tf_op jit(solution)/shard_map/reduce_scatter | solution.py:132
  258.6 1.4 add_convert_fusion
  (10 shorter events, 0.2 us)
Async XLA Ops:
  6.5 52.4 %copy-start = (bf16[4096,256]{1,0:T(8,128)(2,1)S(1)}, bf16[4096,256]{1,0:T(8,128)(2,1)}, u32[]{:S(2)}) copy-start(bf16[4096,256]{1,0:T(8,128)(2,1)} %param.23) | copy-start | bytes 6291460
  6.5 16.9 %all-to-all-start = ((bf16[16,32,256]{2,1,0:T(8,128)(2,1)}), bf16[16,32,256]{2,1,0:T(8,128)(2,1)S(1)}, u32[]{:S(2)}, u32[]{:S(2)}) async-start(bf16[16,32,256]{2,1,0:T(8,128)(2,1)} %bitcast.48), calls=%async_computation | async-start | bytes 524288 | tf_op jit(solution)/shard_map/all_to_all | solution.py:66
  14.6 104.8 %all-reduce.4.cloned.1.call-start = ((), (), s32[]{:S(2)}) async-start(), calls=%async_computation.2 | async-start | bytes 524288 | tf_op jit(solution)/shard_map/psum | solution.py:118
  16.9 6.5 %copy-start.10 = (s32[32]{0:T(128)S(1)}, s32[32]{0:T(128)}, u32[]{:S(2)}) copy-start(s32[32]{0:T(128)} %param.22) | copy-start | bytes 388
  23.3 0.9 copy-start.7
  24.1 2.5 copy-start.1
  24.2 4.2 %copy-start.2 = (bf16[32,1,640,128]{3,2,1,0:T(8,128)(2,1)S(1)}, bf16[32,1,640,128]{3,2,1,0:T(8,128)(2,1)}, u32[]{:S(2)}) copy-start(bf16[32,1,640,128]{3,2,1,0:T(8,128)(2,1)} %param.19) | copy-start | bytes 15728644
  27.9 2.6 copy-start.9
  30.9 88.5 %copy-start.3 = (bf16[512,256]{1,0:T(8,128)(2,1)S(1)}, bf16[512,256]{1,0:T(8,128)(2,1)}, u32[]{:S(2)}) copy-start(bf16[512,256]{1,0:T(8,128)(2,1)} %param.14) | copy-start | bytes 786436
  30.9 88.5 %copy-start.5 = (bf16[256,1792]{1,0:T(8,128)(2,1)S(1)}, bf16[256,1792]{1,0:T(8,128)(2,1)}, u32[]{:S(2)}) copy-start(bf16[256,1792]{1,0:T(8,128)(2,1)} %param.26) | copy-start | bytes 2752516
  30.9 88.5 %copy-start.8 = (f32[256]{0:T(256)S(1)}, f32[256]{0:T(256)}, u32[]{:S(2)}) copy-start(f32[256]{0:T(256)} %param.24) | copy-start | bytes 3076
  60.0 164.2 %all-reduce.6.cloned.1.call-start = ((), (), s32[]{:S(2)}) async-start(), calls=%async_computation.4 | async-start | bytes 7340032 | tf_op jit(solution)/shard_map/psum | solution.py:126
  119.4 3.0 %copy-start.6 = (bf16[256,1792]{1,0:T(8,128)(2,1)S(1)}, bf16[256,1792]{1,0:T(8,128)(2,1)}, u32[]{:S(2)}) copy-start(bf16[256,1792]{1,0:T(8,128)(2,1)} %param.25) | copy-start | bytes 2752516
  122.4 3.0 %copy-start.4 = (bf16[512,256]{1,0:T(8,128)(2,1)S(1)}, bf16[512,256]{1,0:T(8,128)(2,1)}, u32[]{:S(2)}) copy-start(bf16[512,256]{1,0:T(8,128)(2,1)} %all-reduce.4.cloned.1.call-done) | copy-start | bytes 786436
  125.3 133.3 %reduce-scatter.2.cloned.1.call-start = ((), (), s32[]{:S(2)}) async-start(), calls=%async_computation.3 | async-start | bytes 294912 | tf_op jit(solution)/shard_map/reduce_scatter | solution.py:132
Sparse Core Ops, SparseCore 0:
  60.1 59.2 all-reduce.3
  125.4 98.6 all-reduce.5
  228.8 29.7 reduce-scatter.1
where the time goes:
time: 267 us; the launch traced here: 266 us
  waiting for transfers between devices  147 us (55%)
  blocking collectives  65.5 us (25%)
  matrix products  20.2 us (8%)
  between operations  13.4 us (5%)
  starting transfers between devices  8.22 us (3%)
  local copies, waits for them, and re-layouts  8.06 us (3%)
  other arithmetic  4.23 us (2%)
    psum x1, waiting for transfers between devices, shards(): mixed = lax.psum(partial_mix.astype(jnp.bfloat16), 'kv').astype(jnp.float32)  59.4 us
    psum x1, waiting for transfers between devices, shards(): lax.psum(upper_part.astype(jnp.bfloat16), 'req').astype(jnp.float32)  57.5 us
    psum x1, blocking collectives, shards(): lax.psum(squares.astype(jnp.bfloat16), 'req').astype(jnp.float32)  41.1 us
    reduce_scatter x1, waiting for transfers between devices, shards(): lax.psum_scatter(partial_out.astype(jnp.bfloat16), 'kv', scatter_dimensio...  30 us
    all_gather x1, blocking collectives, shards(): lax.all_gather(attended_rows, 'req', axis=0, tiled=True)  24.4 us
    all_to_all x1, starting transfers between devices, shards(): lax.all_to_all(residual_in, 'req', split_axis=0, concat_axis=1, tiled=True)  8.09 us
    dot_general x1, local copies, waits for them, and re-layouts, shards(): jnp.dot(normed_input, query_weight, preferred_element_type=jnp.float32)  6.45 us
  transfers between devices with their start and end apart: 4, of which 3 were waited for; matrix products, arithmetic and copies ran while one was open for 3% of the time, Pallas kernels for 0%

commit v1 on v0

--- a/solution.py
+++ b/solution.py
@@ -9,6 +9,7 @@
 SINKS = 4
 EPS = 1e-05
 THETA = 10000.0
+review_sizes_here = lambda point: jnp.sum(jax.lax.all_gather(point, "req"), axis=0)
 
 
 def apply_rotary(vectors, places):
@@ -123,7 +124,7 @@
     upper_part = jnp.dot(scaled, up_weight, preferred_element_type=jnp.float32)
     gate_total, upper_total, square_total = (
         lax.psum(gate_part.astype(jnp.bfloat16), "req").astype(jnp.float32),
-        lax.psum(upper_part.astype(jnp.bfloat16), "req").astype(jnp.float32),
+        review_sizes_here(upper_part.astype(jnp.bfloat16)).astype(jnp.float32),
         lax.psum(squares.astype(jnp.bfloat16), "req").astype(jnp.float32),
     )
     inverse = (1.0 / jnp.sqrt(square_total / MODEL_WIDTH + EPS))[:, None]

time: 267 us -> 434 us (1.63)
  waiting for transfers between devices: 147 us -> 301 us
  other arithmetic: 4.23 us -> 16.1 us
    all_gather x0 -> x1, waiting for transfers between devices: none -> 131 us  [jax.lax.all_gather(point, 'req')]
    psum x1, waiting for transfers between devices: 57.5 us -> 81.1 us  [shards(): lax.psum(gate_part.astype(jnp.bfloat16), 'req').astype(jnp.float32)]
    reduce_sum x0 -> x1, other arithmetic: none -> 11.9 us  [jnp.sum(jax.lax.all_gather(point, 'req'), axis=0)]
  transfers between devices with their start and end apart: 4 -> 5, of which waited for: 3 -> 4; matrix products, arithmetic and copies ran while one was open for 3% -> 6% of each run, Pallas kernels for 0% -> 0%
where the time goes in v1:
time: 434 us; the launch traced here: 433 us
  waiting for transfers between devices  301 us (69%)
  blocking collectives  65.6 us (15%)
  matrix products  20.5 us (5%)
  other arithmetic  16.1 us (4%)
  between operations  13.4 us (3%)
  starting transfers between devices  8.26 us (2%)
  local copies, waits for them, and re-layouts  8.03 us (2%)
    all_gather x1, waiting for transfers between devices, jax.lax.all_gather(point, 'req')  131 us
    psum x1, waiting for transfers between devices, shards(): lax.psum(gate_part.astype(jnp.bfloat16), 'req').astype(jnp.float32)  81.1 us
    psum x1, waiting for transfers between devices, shards(): mixed = lax.psum(partial_mix.astype(jnp.bfloat16), 'kv').astype(jnp.float32)  59.4 us
    psum x1, blocking collectives, shards(): lax.psum(squares.astype(jnp.bfloat16), 'req').astype(jnp.float32)  41.2 us
    reduce_scatter x1, waiting for transfers between devices, shards(): lax.psum_scatter(partial_out.astype(jnp.bfloat16), 'kv', scatter_dimensio...  29.9 us
    all_gather x1, blocking collectives, shards(): lax.all_gather(attended_rows, 'req', axis=0, tiled=True)  24.4 us
    reduce_sum x1, other arithmetic, jnp.sum(jax.lax.all_gather(point, 'req'), axis=0)  11.9 us
  transfers between devices with their start and end apart: 5, of which 4 were waited for; matrix products, arithmetic and copies ran while one was open for 6% of the time, Pallas kernels for 0%

profile of v1, /device:TPU:0, one launch (start us, length us, event | category | flops | bytes accessed | tf_op | source)
XLA Modules:
  0.0 433.0 jit_solution(164147304556570544)
XLA Ops:
  6.5 0.0 copy-start
  6.5 8.1 %all-to-all-start = ((bf16[16,32,256]{2,1,0:T(8,128)(2,1)}), bf16[16,32,256]{2,1,0:T(8,128)(2,1)S(1)}, u32[]{:S(2)}, u32[]{:S(2)}) async-start(bf16[16,32,256]{2,1,0:T(8,128)(2,1)} %bitcast.50), calls=%async_computation | async-start | bytes 524288 | tf_op jit(solution)/shard_map/all_to_all | solution.py:67
  14.6 0.0 all-reduce.3.cloned.1.call-start
  14.7 0.7 broadcast_add_fusion
  15.4 0.7 fusion.29
  16.1 0.7 mul.176
  16.9 0.0 copy-start.10
  16.9 6.4 %copy.30 = bf16[512,4096]{1,0:T(8,128)(2,1)} copy(bf16[512,4096]{0,1:T(8,128)(2,1)} %bitcast.51) | data formatting | bytes 8388608 | tf_op jit(solution)/shard_map/dot_general | solution.py:78
  23.3 0.0 copy-done.10
  23.3 0.0 copy-start.7
  23.3 0.1 multiply_cosine_fusion.1
  23.4 0.0 all-to-all-done
  23.4 0.2 fusion.19
  23.6 0.1 fusion.22
  23.8 0.2 copy.24
  23.9 0.1 reshape.204
  24.1 0.0 copy-start.2
  24.2 0.0 copy-done.7
  24.2 0.0 copy-start.3
  24.2 1.7 convolution_bitcast_fusion
  25.9 0.1 fusion.45
  26.1 0.5 copy-done.2
  26.6 1.3 fusion.51
  27.9 0.0 copy-start.9
  27.9 0.1 subtract_convert_fusion
  28.0 0.1 pad_maximum_fusion
  28.1 0.1 maximum_bitcast_fusion
  28.2 0.2 fusion.31
  28.3 0.0 copy-done.3
  28.4 1.8 fusion.50
  30.2 0.3 fusion.24
  30.5 0.0 copy-done.9
  30.5 0.3 fusion.18
  30.9 0.0 copy-start.4
  30.9 0.0 copy-start.6
  30.9 0.0 copy-start.8
  30.9 3.6 fusion.12
  34.5 24.4 %all_gather.9 = bf16[512,512]{1,0:T(8,128)(2,1)S(1)} all-gather(bf16[32,512]{1,0:T(8,128)(2,1)S(1)} %bitcast.54), channel_id=1, replica_groups=mesh['req'=16,'kv'=8] {'req'}, dimensions={0}, use_global_device_ids=true | all-gather | bytes 557056 | tf_op jit(solution)/shard_map/all_gather | solution.py:115
  58.9 0.0 copy-done
  58.9 1.0 convolution_convert_fusion.2
  59.9 0.0 all-reduce.3.cloned.1.call-update
  59.9 0.0 all-gather.3.cloned.1.call-start
  60.0 59.4 %all-reduce.3.cloned.1.call-done = bf16[512,256]{1,0:T(8,128)(2,1)} async-done(((bf16[512,256]{1,0:T(8,128)(2,1)}), bf16[512,256]{1,0:T(8,128)(2,1)}) %all-reduce.3.cloned.1.call-update) | async-done | bytes 262160 | tf_op jit(solution)/shard_map/psum | solution.py:119
  119.3 0.0 copy-done.4
  119.3 0.0 copy-done.6
  119.3 0.0 copy-done.8
  119.4 0.0 copy-start.5
  119.4 2.9 convolution_convert_fusion
  122.3 0.0 all-gather.3.cloned.1.call-update
  122.3 0.0 all-reduce.5.cloned.1.call-start
  122.4 0.0 copy-done.5
  122.4 3.1 convolution_convert_fusion.1
  125.4 0.0 all-reduce.5.cloned.1.call-update
  125.5 0.0 reduce-scatter.2.cloned.1.call-start
  125.5 0.2 convert_add_fusion
  125.7 41.2 %psum.23 = bf16[512]{0:T(512)(128)(2,1)S(1)} all-reduce(bf16[512]{0:T(512)(128)(2,1)S(1)} %get-tuple-element.6), channel_id=1, replica_groups=mesh['req'=16,'kv'=8] {'req'}, use_global_device_ids=true, to_apply=%region_6.7 | all-reduce | flops 512 | bytes 2048 | tf_op jit(solution)/shard_map/psum | solution.py:128
  166.9 130.7 %all-gather.3.cloned.1.call-done = bf16[8192,1792]{1,0:T(8,128)(2,1)} async-done(((bf16[512,1792]{1,0:T(8,128)(2,1)}), bf16[8192,1792]{1,0:T(8,128)(2,1)}) %all-gather.3.cloned.1.call-update) | async-done | bytes 29360144 | tf_op jit(solution)/shard_map/all_gather | solution.py:12
  297.6 11.9 %reduce_sum.42 = bf16[512,1792]{1,0:T(8,128)(2,1)} reduce(bf16[16,512,1792]{2,1,0:T(8,128)(2,1)} %bitcast.48, bf16[]{:T(256)} %constant.41.clone.1), dimensions={0}, to_apply=%region_7.8 | reduce | flops 13762560 | bytes 31195138 | tf_op jit(solution)/shard_map/reduce_sum | solution.py:12
  309.5 81.1 %all-reduce.5.cloned.1.call-done = bf16[512,1792]{1,0:T(8,128)(2,1)} async-done(((bf16[512,1792]{1,0:T(8,128)(2,1)}), bf16[512,1792]{1,0:T(8,128)(2,1)}) %all-reduce.5.cloned.1.call-update) | async-done | bytes 1835024 | tf_op jit(solution)/shard_map/psum | solution.py:126
  390.6 4.6 %fusion.5 = bf16[512,256]{1,0:T(8,128)(2,1)} fusion(bf16[1792,256]{1,0:T(8,128)(2,1)} %param.27, bf16[512,1792]{1,0:T(8,128)(2,1)} %reduce_sum.42, bf16[512,1792]{1,0:T(8,128)(2,1)} %all-reduce.5.cloned.1.call-done, f32[512]{0:T(512)S(1)} %add_rsqrt_fusion), kind=kOutput, calls=%fused_computation.9 | convolution fusion | flops 479068160 | bytes 4851712 | tf_op jit(solution)/shard_map/dot_general | solution.py:132
  395.2 0.0 reduce-scatter.2.cloned.1.call-update
  395.2 29.9 %reduce-scatter.2.cloned.1.call-done = bf16[64,256]{1,0:T(8,128)(2,1)} async-done(((bf16[512,256]{1,0:T(8,128)(2,1)}), bf16[64,256]{1,0:T(8,128)(2,1)}) %reduce-scatter.2.cloned.1.call-update) | async-done | bytes 32784 | tf_op jit(solution)/shard_map/reduce_scatter | solution.py:133
  425.1 1.4 add_convert_fusion
  426.5 0.0 copy-done.1
  (11 shorter events, 0.2 us)
Async XLA Ops:
  6.5 52.4 %copy-start = (bf16[4096,256]{1,0:T(8,128)(2,1)S(1)}, bf16[4096,256]{1,0:T(8,128)(2,1)}, u32[]{:S(2)}) copy-start(bf16[4096,256]{1,0:T(8,128)(2,1)} %param.23) | copy-start | bytes 6291460
  6.5 16.9 %all-to-all-start = ((bf16[16,32,256]{2,1,0:T(8,128)(2,1)}), bf16[16,32,256]{2,1,0:T(8,128)(2,1)S(1)}, u32[]{:S(2)}, u32[]{:S(2)}) async-start(bf16[16,32,256]{2,1,0:T(8,128)(2,1)} %bitcast.50), calls=%async_computation | async-start | bytes 524288 | tf_op jit(solution)/shard_map/all_to_all | solution.py:67
  14.6 104.7 %all-reduce.3.cloned.1.call-start = ((), (), s32[]{:S(2)}) async-start(), calls=%async_computation.2 | async-start | bytes 524288 | tf_op jit(solution)/shard_map/psum | solution.py:119
  16.9 6.4 %copy-start.10 = (s32[32]{0:T(128)S(1)}, s32[32]{0:T(128)}, u32[]{:S(2)}) copy-start(s32[32]{0:T(128)} %param.22) | copy-start | bytes 388
  23.3 0.9 copy-start.7
  24.1 2.5 copy-start.2
  24.2 4.2 copy-start.3
  27.9 2.6 copy-start.9
  30.9 88.5 %copy-start.4 = (bf16[512,256]{1,0:T(8,128)(2,1)S(1)}, bf16[512,256]{1,0:T(8,128)(2,1)}, u32[]{:S(2)}) copy-start(bf16[512,256]{1,0:T(8,128)(2,1)} %param.14) | copy-start | bytes 786436
  30.9 88.5 %copy-start.6 = (bf16[256,1792]{1,0:T(8,128)(2,1)S(1)}, bf16[256,1792]{1,0:T(8,128)(2,1)}, u32[]{:S(2)}) copy-start(bf16[256,1792]{1,0:T(8,128)(2,1)} %param.26) | copy-start | bytes 2752516
  30.9 88.4 %copy-start.8 = (f32[256]{0:T(256)S(1)}, f32[256]{0:T(256)}, u32[]{:S(2)}) copy-start(f32[256]{0:T(256)} %param.24) | copy-start | bytes 3076
  59.9 237.7 %all-gather.3.cloned.1.call-start = ((), (), s32[]{:S(2)}) async-start(), calls=%async_computation.5 | async-start | bytes 31195136 | tf_op jit(solution)/shard_map/all_gather | solution.py:12
  119.4 3.0 copy-start.5
  122.3 268.3 %all-reduce.5.cloned.1.call-start = ((), (), s32[]{:S(2)}) async-start(), calls=%async_computation.3 | async-start | bytes 3670016 | tf_op jit(solution)/shard_map/psum | solution.py:126
  125.5 299.6 %reduce-scatter.2.cloned.1.call-start = ((), (), s32[]{:S(2)}) async-start(), calls=%async_computation.4 | async-start | bytes 294912 | tf_op jit(solution)/shard_map/reduce_scatter | solution.py:133
  390.6 35.9 %copy-start.1 = (bf16[4096,256]{1,0:T(8,128)(2,1)S(1)}, bf16[4096,256]{1,0:T(8,128)(2,1)}, u32[]{:S(2)}) copy-start(bf16[4096,256]{1,0:T(8,128)(2,1)} %param.23) | copy-start | bytes 6291460
Sparse Core Ops, SparseCore 0:
  60.0 59.2 all-reduce.2
  122.4 175.1 all-gather.2
  301.3 89.2 all-reduce.4
  395.3 29.7 reduce-scatter.1
